TPU v7x, 32 devices: a whole 2x2x4 slice. The times are simulated.
32 devices in a mesh: wide: 16 (over z, y, x), narrow: 2 (over core).
Axes of the slice: x: 2, y: 2, z: 4, core: 2. Of those that a mesh axis runs over, the one named last changes fastest.
Arguments:
- queries: bfloat16 [4096, 768], P(('wide', 'narrow')), may hold values from -40 to 40
- table: bfloat16 [2048, 768], P('wide'), may hold values from -6 to 6
- head: bfloat16 [768, 768], replicated, may hold values from -0.21875 to 0.21875
- pos_ids: int32 [4096], P(('wide', 'narrow')), may hold values from 0 to 2047, as said below
- neg_ids: int32 [4096, 8], P(('wide', 'narrow')), may hold values from 0 to 2047, as said below
- loss_weights: float32 [4096], P(('wide', 'narrow')), may hold values from 8 to 64
Outputs:
- d_queries: float32 [4096, 768], P(('wide', 'narrow'))
- d_table: float32 [2048, 768], P(('wide', 'narrow'))
- d_head: float32 [768, 768], replicated
Inputs may be any that keep to these rules, and one draw needn't show every extreme that they name: `pos_ids`: the queries form aligned blocks of 128 (the queries of one device). Within a block at most 16 positives lie in one shard of 128 consecutive passage rows (shard = id // 128); one shard, the same for every block, holds exactly 16 of every block. `neg_ids`: within each aligned block of 128 queries, at most 96 of its 1024 negatives lie in one shard of 128 consecutive passage rows (shard = id // 128); one shard, the same for every block, holds exactly 96 of every block. Popular rows recur.
All inputs are finite; a program needn't handle non-finite values.
Results may differ from a plain program's by a relative error of at most 0.0063.
Values may be sent and summed in bfloat16 or wider, within the bound.
A program may use at most 64 MiB of HBM per device.

v0:
```python
import jax
import jax.numpy as jnp
from jax import lax
from jax.sharding import PartitionSpec as P

BOTH = ("wide", "narrow")


def per_device(queries, table, head, pos_ids, neg_ids, loss_weights):
    wide_count = lax.axis_size("wide")
    narrow_count = lax.axis_size("narrow")
    width = queries.shape[1]
    shard_rows = table.shape[0]
    part_rows = shard_rows // narrow_count
    rows = shard_rows * wide_count
    scale = float(width) ** (-0.5)
    mine = lax.axis_index("narrow")
    my_table = lax.dynamic_slice_in_dim(table, mine * part_rows, part_rows, 0)
    my_proj = jnp.dot(my_table, head, preferred_element_type=jnp.float32).astype(jnp.bfloat16)
    table_proj = lax.all_gather(my_proj, BOTH, axis=0, tiled=True)
    group_pos = lax.all_gather(pos_ids, "narrow", axis=0, tiled=True)
    query_proj = jnp.dot(queries, head, preferred_element_type=jnp.float32).astype(jnp.bfloat16)
    columns = jnp.arange(rows, dtype=jnp.int32)
    key_count = jnp.sum((group_pos[:, None] == columns[None, :]).astype(jnp.float32), axis=0)
    own = (pos_ids[:, None] == columns[None, :]).astype(jnp.float32)
    count = jnp.broadcast_to(key_count[None, :], own.shape)
    for n in range(neg_ids.shape[1]):
        count = count + (neg_ids[:, n : n + 1] == columns[None, :]).astype(jnp.float32)
    scores = (
        lax.dot_general(
            query_proj, table_proj, (((1,), (1,)), ((), ())), preferred_element_type=jnp.float32
        )
        * scale
    )
    top = jnp.max(jnp.where(count > 0, scores, -jnp.inf), axis=1, keepdims=True)
    exps = jnp.where(count > 0, jnp.exp(jnp.minimum(scores - top, 0.0)), 0.0)
    total = jnp.sum(count * exps, axis=1, keepdims=True)
    probs = exps / total
    weight = loss_weights[:, None] * scale
    coef = (weight * probs).astype(jnp.bfloat16).astype(jnp.float32)
    own_coef = (weight * (probs - 1.0)).astype(jnp.bfloat16).astype(jnp.float32)
    coef = ((count - own) * coef + own * own_coef).astype(jnp.bfloat16)
    grad_query = jnp.dot(coef, table_proj, preferred_element_type=jnp.float32).astype(jnp.bfloat16)
    d_queries = lax.dot_general(
        grad_query, head, (((1,), (1,)), ((), ())), preferred_element_type=jnp.float32
    )
    row_partial = lax.dot_general(
        coef, query_proj, (((0,), (0,)), ((), ())), preferred_element_type=jnp.float32
    ).astype(jnp.bfloat16)
    pieces = lax.all_to_all(row_partial, BOTH, split_axis=0, concat_axis=0, tiled=True)
    row_grad = jnp.sum(pieces.reshape(-1, part_rows, width).astype(jnp.float32), axis=0)
    row_grad = row_grad.astype(jnp.bfloat16)
    d_table = lax.dot_general(
        row_grad, head, (((1,), (1,)), ((), ())), preferred_element_type=jnp.float32
    )
    head_part = lax.dot_general(
        queries, grad_query, (((0,), (0,)), ((), ())), preferred_element_type=jnp.float32
    )
    head_part = head_part + lax.dot_general(
        my_table, row_grad, (((0,), (0,)), ((), ())), preferred_element_type=jnp.float32
    )
    d_head = lax.psum(head_part, BOTH)
    return (d_queries, d_table, d_head)


def solution(mesh):
    placed = (P(BOTH, None), P("wide", None), P(), P(BOTH), P(BOTH, None), P(BOTH))
    return jax.shard_map(
        per_device,
        mesh=mesh,
        in_specs=placed,
        out_specs=(P(BOTH, None), P(BOTH, None), P()),
        check_vma=False,
    )
```

profile of v0, /device:TPU:0, one launch (start us, length us, event | category | flops | bytes accessed | tf_op | source)
XLA Modules:
  0.0 308.6 jit_solution(17481606412836012648)
XLA Ops:
  7.2 0.0 copy-start
  7.2 0.0 all-gather.3.cloned.1.call-start
  7.2 1.2 copy-done
  8.4 1.9 convolution_convert_fusion.3
  10.3 0.0 all-gather.3.cloned.1.call-update
  10.3 2.1 all-gather
  12.4 0.3 convert_reduce_fusion
  12.8 0.7 broadcast_multiply_fusion
  13.4 1.0 slice_bitcast_fusion.7
  14.4 1.2 convolution_convert_fusion.2
  15.7 57.6 %all-gather.3.cloned.1.call-done = bf16[2048,768]{1,0:T(8,128)(2,1)} async-done(((bf16[64,768]{1,0:T(8,128)(2,1)}), bf16[2048,768]{1,0:T(8,128)(2,1)}) %all-gather.3.cloned.1.call-update) | async-done | bytes 3145744 | tf_op jit(solution)/shard_map/all_gather | solution.py:20
  73.3 0.0 copy-start.5
  73.3 3.7 %select_reduce_fusion = (f32[128]{0:T(128)S(1)}, f32[128,2048]{1,0:T(8,128)S(1)}) fusion(s32[128]{0:T(128)S(1)} %get-tuple-element.18, s32[128]{0:T(128)S(1)} %get-tuple-element.19, s32[128]{0:T(128)S(1)} %get-tuple-element.13, s32[128]{0:T(128)S(1)} %get-tuple-element.14, s32[128]{0:T(128)S(1)} %get-tuple-element.15, s32[128]{0:T(128)S(1)} %get-tuple-element.16, ...), kind=kOutput, calls=%fused_computation.13 | convolution fusion | flops 409993088 | bytes 4403712 | tf_op jit(solution)/shard_map/dot_general | solution.py:30
  77.0 1.5 multiply_reduce_fusion
  78.5 0.0 copy-done.5
  78.5 4.2 %convolution_convert_fusion = bf16[2048,768]{1,0:T(8,128)(2,1)} fusion(bf16[128,768]{1,0:T(8,128)(2,1)S(1)} %convolution_convert_fusion.2, f32[128,2048]{1,0:T(8,128)S(1)} %get-tuple-element.21, f32[128]{0:T(128)S(1)} %multiply_reduce_fusion, f32[128]{0:T(128)S(1)} %get-tuple-element.20, f32[128]{0:T(128)S(1)} %broadcast_multiply_fusion, ...), kind=kOutput, calls=%fused_computation | convolution fusion | flops 415498240 | bytes 4405248 | tf_op jit(solution)/shard_map/dot_general | solution.py:47
  82.8 3.5 %all-to-all-start = ((bf16[32,64,768]{2,1,0:T(8,128)(2,1)}), bf16[32,64,768]{2,1,0:T(8,128)(2,1)}, u32[]{:S(2)}, u32[]{:S(2)}) async-start(bf16[32,64,768]{2,1,0:T(8,128)(2,1)} %bitcast.35), calls=%async_computation | async-start | bytes 6291456 | tf_op jit(solution)/shard_map/all_to_all | solution.py:50
  86.3 0.0 all-reduce.2.cloned.1.call-start
  86.3 0.0 copy-start.2
  86.3 4.1 %convolution_convert_fusion.1 = bf16[128,768]{1,0:T(8,128)(2,1)S(1)} fusion(bf16[2048,768]{1,0:T(8,128)(2,1)} %all-gather.3.cloned.1.call-done, f32[128,2048]{1,0:T(8,128)S(1)} %get-tuple-element.21, f32[128]{0:T(128)S(1)} %multiply_reduce_fusion, f32[128]{0:T(128)S(1)} %get-tuple-element.20, f32[128]{0:T(128)S(1)} %broadcast_multiply_fusion, ...), kind=kOutput, calls=%fused_computation.5 | convolution fusion | flops 414023680 | bytes 4405248 | tf_op jit(solution)/shard_map/dot_general | solution.py:43
  90.4 0.0 copy-start.3
  90.4 0.7 copy-done.3
  91.1 0.0 copy-done.2
  91.1 0.5 fusion.7
  91.6 66.1 %all-to-all-done = bf16[32,64,768]{2,1,0:T(8,128)(2,1)} async-done(((bf16[32,64,768]{2,1,0:T(8,128)(2,1)}), bf16[32,64,768]{2,1,0:T(8,128)(2,1)}, u32[]{:S(2)}, u32[]{:S(2)}) %all-to-all-start) | async-done | bytes 3145760 | tf_op jit(solution)/shard_map/all_to_all | solution.py:50
  157.7 3.0 reduce_sum.32
  160.7 2.9 bitcast_add_fusion
  163.5 0.0 copy-start.4
  163.5 0.0 copy-start.1
  163.5 0.0 all-reduce.2.cloned.1.call-update
  163.5 0.9 copy-done.4
  164.4 1.3 fusion.5
  165.7 0.0 copy-done.1
  165.7 1.2 fusion.6
  166.9 131.8 %all-reduce.2.cloned.1.call-done = f32[768,768]{0,1:T(8,128)} async-done(((f32[768,768]{0,1:T(8,128)}), f32[768,768]{0,1:T(8,128)}) %all-reduce.2.cloned.1.call-update) | async-done | bytes 2359312 | tf_op jit(solution)/shard_map/psum | solution.py:62
  298.7 3.0 copy.14
Async XLA Ops:
  7.2 1.3 copy-start
  7.2 66.1 %all-gather.3.cloned.1.call-start = ((), (), s32[]{:S(2)}) async-start(), calls=%async_computation.1 | async-start | bytes 3244032 | tf_op jit(solution)/shard_map/all_gather | solution.py:20
  73.3 5.2 %copy-start.5 = (s32[128]{0:T(128)S(1)}, s32[128]{0:T(128)}, u32[]{:S(2)}) copy-start(s32[128]{0:T(128)} %param.9) | copy-start | bytes 1540
  82.8 74.9 %all-to-all-start = ((bf16[32,64,768]{2,1,0:T(8,128)(2,1)}), bf16[32,64,768]{2,1,0:T(8,128)(2,1)}, u32[]{:S(2)}, u32[]{:S(2)}) async-start(bf16[32,64,768]{2,1,0:T(8,128)(2,1)} %bitcast.35), calls=%async_computation | async-start | bytes 6291456 | tf_op jit(solution)/shard_map/all_to_all | solution.py:50
  86.3 212.4 %all-reduce.2.cloned.1.call-start = ((), (), s32[]{:S(2)}) async-start(), calls=%async_computation.2 | async-start | bytes 4718592 | tf_op jit(solution)/shard_map/psum | solution.py:62
  86.3 4.8 %copy-start.2 = (bf16[128,768]{1,0:T(8,128)(2,1)S(1)}, bf16[128,768]{1,0:T(8,128)(2,1)}, u32[]{:S(2)}) copy-start(bf16[128,768]{1,0:T(8,128)(2,1)} %param.6) | copy-start | bytes 589828
  90.4 0.7 copy-start.3
  163.5 0.9 copy-start.4
  163.5 2.2 copy-start.1
Sparse Core Ops, SparseCore 0:
  11.4 61.7 all-gather.2
  163.7 135.0 all-reduce.1
where the time goes:
time: 309 us
  waiting for transfers between devices  256 us (83%)
  matrix products  20.9 us (7%)
  between operations  14.1 us (5%)
  local copies, waits for them, and re-layouts  6.83 us (2%)
  other arithmetic  5.46 us (2%)
  starting transfers between devices  3.6 us (1%)
    psum x1, waiting for transfers between devices, per_device(): d_head = lax.psum(head_part, BOTH)  132 us
    all_to_all x1, waiting for transfers between devices, per_device(): lax.all_to_all(row_partial, BOTH, split_axis=0, concat_axis=0, tiled=True)  66.1 us
    all_gather x1, waiting for transfers between devices, per_device(): table_proj = lax.all_gather(my_proj, BOTH, axis=0, tiled=True)  57.6 us
  transfers between devices with their start and end apart: 3, of which 3 were waited for; matrix products, arithmetic and copies ran while one was open for 3% of the time, Pallas kernels for 0%

commit v1 on v0

--- a/solution.py
+++ b/solution.py
@@ -4,6 +4,7 @@
 from jax.sharding import PartitionSpec as P
 
 BOTH = ("wide", "narrow")
+_divide_groups = lambda x_in, lane_axis, axis_name: lax.psum(lax.psum(x_in, lane_axis), axis_name)
 
 
 def per_device(queries, table, head, pos_ids, neg_ids, loss_weights):
@@ -59,7 +60,7 @@
     head_part = head_part + lax.dot_general(
         my_table, row_grad, (((0,), (0,)), ((), ())), preferred_element_type=jnp.float32
     )
-    d_head = lax.psum(head_part, BOTH)
+    d_head = _divide_groups(head_part, "narrow", "wide")
     return (d_queries, d_table, d_head)
 
 

time: 309 us -> 333 us (1.078)
  waiting for transfers between devices: 256 us -> 281 us
    psum x1 -> x2, waiting for transfers between devices: 132 us -> 157 us  [the longest x1 136 us: lax.psum(lax.psum(x_in, lane_axis), axis_name)]
  transfers between devices with their start and end apart: 3 -> 4, of which waited for: 3 -> 4; matrix products, arithmetic and copies ran while one was open for 3% -> 3% of each run, Pallas kernels for 0% -> 0%
where the time goes in v1:
time: 333 us
  waiting for transfers between devices  281 us (84%)
  matrix products  21 us (6%)
  between operations  13.8 us (4%)
  local copies, waits for them, and re-layouts  5.93 us (2%)
  other arithmetic  5.47 us (2%)
  starting transfers between devices  3.65 us (1%)
    psum x1, waiting for transfers between devices, lax.psum(lax.psum(x_in, lane_axis), axis_name)  136 us
    all_to_all x1, waiting for transfers between devices, per_device(): lax.all_to_all(row_partial, BOTH, split_axis=0, concat_axis=0, tiled=True)  66.1 us
    all_gather x1, waiting for transfers between devices, per_device(): table_proj = lax.all_gather(my_proj, BOTH, axis=0, tiled=True)  57.6 us
    psum x1, waiting for transfers between devices, lax.psum(x_in, lane_axis)  21.2 us
  transfers between devices with their start and end apart: 4, of which 4 were waited for; matrix products, arithmetic and copies ran while one was open for 3% of the time, Pallas kernels for 0%

profile of v1, /device:TPU:0, one launch (start us, length us, event | category | flops | bytes accessed | tf_op | source)
XLA Modules:
  0.0 332.7 jit_solution(11036797139654866939)
XLA Ops:
  7.2 0.0 copy-start
  7.2 0.0 all-gather.3.cloned.1.call-start
  7.2 1.2 copy-done
  8.4 1.9 convolution_convert_fusion.3
  10.3 0.0 all-gather.3.cloned.1.call-update
  10.3 2.1 all-gather
  12.4 0.3 convert_reduce_fusion
  12.8 0.7 broadcast_multiply_fusion
  13.4 1.0 slice_bitcast_fusion.7
  14.4 1.2 convolution_convert_fusion.2
  15.7 57.6 %all-gather.3.cloned.1.call-done = bf16[2048,768]{1,0:T(8,128)(2,1)} async-done(((bf16[64,768]{1,0:T(8,128)(2,1)}), bf16[2048,768]{1,0:T(8,128)(2,1)}) %all-gather.3.cloned.1.call-update) | async-done | bytes 3145744 | tf_op jit(solution)/shard_map/all_gather | solution.py:21
  73.3 0.0 copy-start.5
  73.3 3.7 %select_reduce_fusion = (f32[128]{0:T(128)S(1)}, f32[128,2048]{1,0:T(8,128)S(1)}) fusion(s32[128]{0:T(128)S(1)} %get-tuple-element.18, s32[128]{0:T(128)S(1)} %get-tuple-element.19, s32[128]{0:T(128)S(1)} %get-tuple-element.13, s32[128]{0:T(128)S(1)} %get-tuple-element.14, s32[128]{0:T(128)S(1)} %get-tuple-element.15, s32[128]{0:T(128)S(1)} %get-tuple-element.16, ...), kind=kOutput, calls=%fused_computation.13 | convolution fusion | flops 409993088 | bytes 4403712 | tf_op jit(solution)/shard_map/dot_general | solution.py:31
  77.0 1.5 multiply_reduce_fusion
  78.5 0.0 copy-done.5
  78.5 4.2 %convolution_convert_fusion = bf16[2048,768]{1,0:T(8,128)(2,1)} fusion(bf16[128,768]{1,0:T(8,128)(2,1)S(1)} %convolution_convert_fusion.2, f32[128,2048]{1,0:T(8,128)S(1)} %get-tuple-element.21, f32[128]{0:T(128)S(1)} %multiply_reduce_fusion, f32[128]{0:T(128)S(1)} %get-tuple-element.20, f32[128]{0:T(128)S(1)} %broadcast_multiply_fusion, ...), kind=kOutput, calls=%fused_computation | convolution fusion | flops 415498240 | bytes 4405248 | tf_op jit(solution)/shard_map/dot_general | solution.py:48
  82.8 3.5 %all-to-all-start = ((bf16[32,64,768]{2,1,0:T(8,128)(2,1)}), bf16[32,64,768]{2,1,0:T(8,128)(2,1)}, u32[]{:S(2)}, u32[]{:S(2)}) async-start(bf16[32,64,768]{2,1,0:T(8,128)(2,1)} %bitcast.35), calls=%async_computation | async-start | bytes 6291456 | tf_op jit(solution)/shard_map/all_to_all | solution.py:51
  86.3 0.0 all-reduce.3.cloned.1.call-start
  86.3 0.0 copy-start.2
  86.3 4.1 %convolution_convert_fusion.1 = bf16[128,768]{1,0:T(8,128)(2,1)S(1)} fusion(bf16[2048,768]{1,0:T(8,128)(2,1)} %all-gather.3.cloned.1.call-done, f32[128,2048]{1,0:T(8,128)S(1)} %get-tuple-element.21, f32[128]{0:T(128)S(1)} %multiply_reduce_fusion, f32[128]{0:T(128)S(1)} %get-tuple-element.20, f32[128]{0:T(128)S(1)} %broadcast_multiply_fusion, ...), kind=kOutput, calls=%fused_computation.5 | convolution fusion | flops 414023680 | bytes 4405248 | tf_op jit(solution)/shard_map/dot_general | solution.py:44
  90.4 0.0 copy-start.3
  90.4 0.7 copy-done.3
  91.1 0.0 copy-done.2
  91.1 0.5 fusion.7
  91.6 66.1 %all-to-all-done = bf16[32,64,768]{2,1,0:T(8,128)(2,1)} async-done(((bf16[32,64,768]{2,1,0:T(8,128)(2,1)}), bf16[32,64,768]{2,1,0:T(8,128)(2,1)}, u32[]{:S(2)}, u32[]{:S(2)}) %all-to-all-start) | async-done | bytes 3145760 | tf_op jit(solution)/shard_map/all_to_all | solution.py:51
  157.7 3.0 reduce_sum.32
  160.7 2.9 bitcast_add_fusion
  163.5 0.0 copy-start.4
  163.5 0.0 all-reduce.3.cloned.1.call-update
  163.5 0.0 copy-start.1
  163.5 0.0 all-reduce.5.cloned.1.call-start
  163.6 21.2 %all-reduce.3.cloned.1.call-done = f32[768,768]{0,1:T(8,128)} async-done(((f32[768,768]{0,1:T(8,128)}), f32[768,768]{0,1:T(8,128)}) %all-reduce.3.cloned.1.call-update) | async-done | bytes 2359312 | tf_op jit(solution)/shard_map/psum | solution.py:7
  184.8 0.0 all-reduce.5.cloned.1.call-update
  184.8 0.0 copy-done.4
  184.8 1.3 fusion.5
  186.1 0.0 copy-done.1
  186.1 1.2 fusion.6
  187.3 135.8 %all-reduce.5.cloned.1.call-done = f32[768,768]{0,1:T(8,128)} async-done(((f32[768,768]{0,1:T(8,128)}), f32[768,768]{0,1:T(8,128)}) %all-reduce.5.cloned.1.call-update) | async-done | bytes 2359312 | tf_op jit(solution)/shard_map/psum | solution.py:7
  323.1 3.0 copy.14
Async XLA Ops:
  7.2 1.3 copy-start
  7.2 66.1 %all-gather.3.cloned.1.call-start = ((), (), s32[]{:S(2)}) async-start(), calls=%async_computation.1 | async-start | bytes 3244032 | tf_op jit(solution)/shard_map/all_gather | solution.py:21
  73.3 5.2 %copy-start.5 = (s32[128]{0:T(128)S(1)}, s32[128]{0:T(128)}, u32[]{:S(2)}) copy-start(s32[128]{0:T(128)} %param.9) | copy-start | bytes 1540
  82.8 74.9 %all-to-all-start = ((bf16[32,64,768]{2,1,0:T(8,128)(2,1)}), bf16[32,64,768]{2,1,0:T(8,128)(2,1)}, u32[]{:S(2)}, u32[]{:S(2)}) async-start(bf16[32,64,768]{2,1,0:T(8,128)(2,1)} %bitcast.35), calls=%async_computation | async-start | bytes 6291456 | tf_op jit(solution)/shard_map/all_to_all | solution.py:51
  86.3 98.5 %all-reduce.3.cloned.1.call-start = ((), (), s32[]{:S(2)}) async-start(), calls=%async_computation.2 | async-start | bytes 4718592 | tf_op jit(solution)/shard_map/psum | solution.py:7
  86.3 4.8 %copy-start.2 = (bf16[128,768]{1,0:T(8,128)(2,1)S(1)}, bf16[128,768]{1,0:T(8,128)(2,1)}, u32[]{:S(2)}) copy-start(bf16[128,768]{1,0:T(8,128)(2,1)} %param.6) | copy-start | bytes 589828
  90.4 0.7 copy-start.3
  163.5 21.3 %copy-start.4 = (bf16[128,768]{1,0:T(8,128)(2,1)S(1)}, bf16[128,768]{1,0:T(8,128)(2,1)}, u32[]{:S(2)}) copy-start(bf16[128,768]{1,0:T(8,128)(2,1)} %copy-done.3) | copy-start | bytes 589828
  163.5 22.6 %copy-start.1 = (bf16[64,768]{1,0:T(8,128)(2,1)S(1)}, bf16[64,768]{1,0:T(8,128)(2,1)}, u32[]{:S(2)}) copy-start(bf16[64,768]{1,0:T(8,128)(2,1)} %reduce_sum.32) | copy-start | bytes 294916
  163.5 159.6 %all-reduce.5.cloned.1.call-start = ((), (), s32[]{:S(2)}) async-start(), calls=%async_computation.3 | async-start | bytes 4718592 | tf_op jit(solution)/shard_map/psum | solution.py:7
Sparse Core Ops, SparseCore 0:
  11.4 61.7 all-gather.2
  163.7 21.0 all-reduce.2
  190.4 132.6 all-reduce.4
